TPU v7x, 256 devices: a whole 4x4x8 slice. The times are simulated.
256 devices in a mesh: grp: 2 (over core), dom: 64 (over y_lo, z, x), sub: 2 (over y_hi).
Axes of the slice: x: 4, y: 4 (y_hi: 2, y_lo: 2; y = y_hi * 2 + y_lo), z: 8, core: 2. Of those that a mesh axis runs over, the one named last changes fastest.
Arguments:
- positions: float32 [3, 65536], P(None, ('grp', 'dom', 'sub')), may hold values from 0 to 4
- charges: float32 [65536], P(('grp', 'dom', 'sub')), may hold values from -3 to 3
- polar: float32 [65536], P(('grp', 'dom', 'sub')), may hold values from 0.1 to 0.6
- features: bfloat16 [65536, 256], P(('grp', 'dom', 'sub')), may hold values from -6 to 6
- neighbours: int32 [65536, 32], P(('grp', 'dom', 'sub')), may hold values from 0 to 512, as said below
- send_rows: int32 [2, 32768], P(None, ('grp', 'dom', 'sub')), may hold values from 0 to 255
- blocks: int32 [1024], P(('grp', 'dom', 'sub')), may hold values from 0 to 255
- radial_in: bfloat16 [2, 8, 64], replicated, may hold values from -2 to 2
- radial_mid: bfloat16 [2, 2, 64, 64], replicated, may hold values from -0.75 to 0.75
- radial_out: bfloat16 [2, 64, 256], replicated, may hold values from -0.75 to 0.75
- node_in: bfloat16 [2, 256, 256], replicated, may hold values from -0.375 to 0.375
- node_out: bfloat16 [2, 256, 256], replicated, may hold values from -0.375 to 0.375
- field_gain: float32 [256], replicated, may hold values from -3 to 3
- readout: bfloat16 [256, 2], replicated, may hold values from -0.375 to 0.375
Outputs:
- site_result: float32 [3, 65536], P(None, ('grp', 'dom', 'sub'))
- response: float32 [3, 65536], P(None, ('grp', 'dom', 'sub'))
Inputs may be any that keep to these rules, and one draw needn't show every extreme that they name: `neighbours`: entries below 256 name the block's own sites, entries from 256 to 511 its lent sites, 512 an empty slot; empty slots follow the used ones. `blocks`: repeats may occur.
All inputs are finite; a program needn't handle non-finite values.
Results may differ from a plain program's by a relative error of at most 0.0022.
The roundings to bfloat16 on the way count: a program that leaves them out, or rounds other values in their place, can miss the bound.
Values may be sent and summed in bfloat16 or wider, within the bound.
No kernel may reach another device: no remote copies, remote signals or barrier semaphores. Data moves between devices by JAX's collectives and lax.ppermute only.
A program may use at most 64 MiB of HBM per device.

v0:
```python
import jax
import jax.numpy as jnp
from jax import lax
from jax.sharding import PartitionSpec as P

BASIS = 8
LAYERS = 2
SWEEPS = 4
BLOCK = 128
SMOOTH = 1.0
GAMMA = 1.0
SPACING = 0.75


def with_halo(block, sides, width):
    for axis, dim in sides:
        count = lax.axis_size(axis)
        forward = [(i, i + 1) for i in range(count - 1)]
        backward = [(target, source) for source, target in forward]
        low = lax.ppermute(
            lax.slice_in_dim(block, block.shape[dim] - width, None, axis=dim), axis, forward
        )
        high = lax.ppermute(lax.slice_in_dim(block, 0, width, axis=dim), axis, backward)
        block = jnp.concatenate([low, block, high], axis=dim)
    return block


def partner_2(value, axis, bit):
    mask = 2**bit
    pairs = [(source, source ^ mask) for source in range(lax.axis_size(axis))]
    return lax.ppermute(value, axis, pairs)


def field_at(target, source, charge, dipole):
    tile_count = target.shape[1] // BLOCK
    tiles = target.reshape(3, tile_count, BLOCK).transpose(1, 0, 2)

    def field_one_tile(target_tile):
        offset = target_tile[:, :, None] - source[:, None, :]
        dist_sq = jnp.sum(offset * offset, axis=0) + SMOOTH
        inverse = lax.rsqrt(dist_sq)
        inverse_cube = inverse * inverse * inverse
        inverse_fifth = inverse_cube * inverse * inverse
        projected = jnp.sum(offset * dipole[:, None, :], axis=0)
        source_scale = charge[None, :] * inverse_cube + 3.0 * projected * inverse_fifth
        return jnp.sum(
            offset * source_scale[None] - dipole[:, None, :] * inverse_cube[None], axis=2
        )

    return lax.map(field_one_tile, tiles).transpose(1, 0, 2).reshape(3, -1)


def slot_field(offset, dist_sq, source_charge, source_dipole):
    inverse = lax.rsqrt(dist_sq)
    inverse_cube = inverse * inverse * inverse
    inverse_fifth = inverse_cube * inverse * inverse
    projected = jnp.sum(offset * source_dipole, axis=0)
    source_scale = source_charge * inverse_cube + 3.0 * projected * inverse_fifth
    return jnp.sum(offset * source_scale[None] - source_dipole * inverse_cube[None], axis=1)


def message_update(
    hidden, lifted_table, radial_basis, slot_major, w_first, w_middle, w_last, w_node
):
    row_count, channel_count = hidden.shape
    slot_count = slot_major.shape[0]
    basis_width = radial_basis.shape[2]
    tile_count = row_count // BLOCK

    def message_one_tile(tile_index):
        start = tile_index * BLOCK
        basis_tile = lax.dynamic_slice_in_dim(radial_basis, start, BLOCK, 1).reshape(
            slot_count * BLOCK, basis_width
        )
        index_tile = lax.dynamic_slice_in_dim(slot_major, start, BLOCK, 1)
        first_hidden = jax.nn.silu(
            jnp.dot(basis_tile, w_first, preferred_element_type=jnp.float32)
        ).astype(jnp.bfloat16)
        second_hidden = jax.nn.silu(
            jnp.dot(first_hidden, w_middle[0], preferred_element_type=jnp.float32)
        ).astype(jnp.bfloat16)
        third_hidden = jax.nn.silu(
            jnp.dot(second_hidden, w_middle[1], preferred_element_type=jnp.float32)
        ).astype(jnp.bfloat16)
        edge_weight = jnp.dot(third_hidden, w_last, preferred_element_type=jnp.float32).reshape(
            slot_count, BLOCK, channel_count
        )
        source = lifted_table[index_tile].astype(jnp.float32)
        summed = jnp.sum(edge_weight * source, axis=0)
        return summed / slot_count

    message = (
        lax.map(message_one_tile, jnp.arange(tile_count, dtype=jnp.int32))
        .reshape(row_count, channel_count)
        .astype(jnp.bfloat16)
    )
    update = jax.nn.silu(jnp.dot(message, w_node, preferred_element_type=jnp.float32))
    return (hidden.astype(jnp.float32) + update).astype(jnp.bfloat16)


def extend_cols(values, rim_rows, rim_width):
    empty_entry = jnp.zeros(values.shape[:-1] + (1,), values.dtype)
    return jnp.concatenate(
        [values, rim_rows[..., :rim_width], rim_rows[..., 3 * rim_width :], empty_entry], axis=-1
    )


def extend_rows(values, rim_rows, rim_width):
    empty_entry = jnp.zeros((1,) + values.shape[1:], values.dtype)
    return jnp.concatenate(
        [values, rim_rows[:rim_width], rim_rows[3 * rim_width :], empty_entry], axis=0
    )


def local(
    positions,
    charges,
    polar,
    features,
    neighbours,
    send_rows,
    blocks,
    radial_in,
    radial_mid,
    radial_out,
    node_in,
    node_out,
    field_gain,
    readout,
):
    rim_width = send_rows.shape[1]
    row_count = positions.shape[1]
    block_width = BLOCK
    own_blocks = row_count // block_width
    listed_count = blocks.shape[0]
    domain_count = lax.axis_size(("dom", "sub"))
    domain_index = lax.axis_index(("dom", "sub"))
    group_blocks = own_blocks * domain_count
    learned = lax.axis_index("grp") == 0
    slot_major = neighbours.T
    local_data = jnp.concatenate([positions, charges[None], polar[None]], axis=0)
    outgoing = jnp.concatenate([local_data[:, send_rows[1]], local_data[:, send_rows[0]]], axis=1)
    rim_rows = with_halo(outgoing, ((("dom", "sub"), 1),), rim_width)
    site_table = extend_cols(local_data, rim_rows, rim_width)
    partner = partner_2(local_data, "grp", 0)
    others = lax.all_gather(partner, ("dom", "sub"), axis=1, tiled=True)
    near_sites = jnp.take(others.reshape(5, -1, block_width), blocks, axis=1).reshape(5, -1)
    outside = field_at(positions, near_sites[:3], near_sites[3], jnp.zeros_like(near_sites[:3]))
    offset = positions[:, None, :] - site_table[:3][:, slot_major]
    dist_sq = jnp.sum(offset * offset, axis=0) + SMOOTH
    strength = jnp.sqrt(1.0 + jnp.sum(outside * outside, axis=0))
    hidden = (features.astype(jnp.float32) + strength[:, None] * field_gain[None, :]).astype(
        jnp.bfloat16
    )
    centres = jnp.arange(BASIS, dtype=jnp.float32) * SPACING
    radial_basis = jnp.exp(-GAMMA * (jnp.sqrt(dist_sq)[:, :, None] - centres) ** 2).astype(
        jnp.bfloat16
    )
    for layer_index in range(LAYERS):
        lifted = lax.cond(
            learned,
            lambda h: jnp.dot(h, node_in[layer_index], preferred_element_type=jnp.float32).astype(
                jnp.bfloat16
            ),
            lambda h: jnp.zeros_like(h),
            hidden,
        )
        lent = jnp.concatenate([lifted[send_rows[1]], lifted[send_rows[0]]], axis=0)
        lifted_rims = with_halo(lent, ((("dom", "sub"), 0),), rim_width)
        lifted_table = extend_rows(lifted, lifted_rims, rim_width)
        hidden = lax.cond(
            learned,
            lambda h, t: message_update(
                h,
                t,
                radial_basis,
                slot_major,
                radial_in[layer_index],
                radial_mid[layer_index],
                radial_out[layer_index],
                node_out[layer_index],
            ),
            lambda h, t: h,
            hidden,
            lifted_table,
        )
    readouts = jnp.dot(hidden, readout, preferred_element_type=jnp.float32)
    charge = readouts[:, 0]
    energy = readouts[:, 1]
    fixed_field = outside + slot_field(
        offset, dist_sq, site_table[3][slot_major], jnp.zeros_like(offset)
    )
    dipole = jnp.where(learned, 0.0, polar[None] * fixed_field)
    for sweep_index in range(SWEEPS):
        lent_dipoles = jnp.concatenate([dipole[:, send_rows[1]], dipole[:, send_rows[0]]], axis=1)
        dipole_rims = with_halo(lent_dipoles, ((("dom", "sub"), 1),), rim_width)
        dipole_table = extend_cols(dipole, dipole_rims, rim_width)
        dipole = lax.cond(
            learned,
            lambda d, t: d,
            lambda d, t: polar[None]
            * (
                fixed_field + slot_field(offset, dist_sq, jnp.zeros_like(dist_sq), t[:, slot_major])
            ),
            dipole,
            dipole_table,
        )
    site_result = jnp.where(learned, jnp.stack([charge, energy, strength]), dipole)
    source_charge = jnp.where(learned, charge, 0.0)
    source_dipole = jnp.where(learned, 0.0, dipole)
    response_term = field_at(near_sites[:3], positions, source_charge, source_dipole)
    scattered = (
        jnp.zeros((3, group_blocks, block_width), jnp.float32)
        .at[:, blocks]
        .add(response_term.reshape(3, listed_count, block_width))
        .reshape(3, -1)
    )
    total = lax.psum(scattered, ("dom", "sub"))
    own_share = lax.dynamic_slice_in_dim(total, domain_index * row_count, row_count, 1)
    response = partner_2(own_share, "grp", 0)
    return (site_result, response)


def solution(mesh):
    in_specs = (
        P(None, ("grp", "dom", "sub")),
        P(("grp", "dom", "sub")),
        P(("grp", "dom", "sub")),
        P(("grp", "dom", "sub"), None),
        P(("grp", "dom", "sub"), None),
        P(None, ("grp", "dom", "sub")),
        P(("grp", "dom", "sub")),
        P(),
        P(),
        P(),
        P(),
        P(),
        P(),
        P(),
    )
    out_specs = (P(None, ("grp", "dom", "sub")), P(None, ("grp", "dom", "sub")))
    return jax.shard_map(local, mesh=mesh, in_specs=in_specs, out_specs=out_specs, check_vma=False)
```

profile of v0, /device:TPU:1, one launch (start us, length us, event | category | flops | bytes accessed | tf_op | source)
XLA Modules:
  0.0 878.2 jit_solution(3538958461297963734)
XLA Ops:
  8.0 3.2 collective-permute-start
  14.7 5.5 collective-permute-start.1
  24.2 32.9 %gather_fusion.14 = f32[8192]{0:T(1024)S(1)} fusion(f32[513]{0:T(1024)S(1)} %slice_reduce_fusion, s32[8192]{0:T(1024)S(1)} %broadcast_clamp_fusion.4), kind=kCustom, calls=%fused_computation.14 | custom fusion | bytes 98304 | tf_op jit(solution)/shard_map/gather | solution.py:191
  57.2 27.9 %gather_fusion.9 = f32[8192,3]{1,0:T(8,128)} fusion(f32[3,513]{0,1:T(8,128)S(1)} %copy.124, s32[8192]{0:T(1024)S(1)} %broadcast_clamp_fusion.4), kind=kCustom, calls=%fused_computation.9 | custom fusion | bytes 229376 | tf_op jit(solution)/shard_map/gather | solution.py:149
  85.1 4.5 multiply_reduce_fusion.4
  89.6 1.9 copy-done.1
  91.5 2.5 subtract_reduce_fusion.4
  94.0 296.4 %all_gather.3 = f32[5,32768]{1,0:T(8,128)S(1)} all-gather(f32[5,256]{1,0:T(8,128)S(1)} %collective-permute-done), channel_id=1, replica_groups=mesh['grp'=2,'dom'=64,'sub'=2] {'dom','sub'}, dimensions={1}, use_global_device_ids=true | all-gather | bytes 660480 | tf_op jit(solution)/shard_map/all_gather | solution.py:146
  395.2 5.5 collective-permute-start.7
  402.1 36.6 %conditional.12 = (f32[3,256]{0,1:T(8,128)S(1)}) conditional(s32[]{:T(128)} %convert_element_type.76, (f32[256]{0:T(256)S(1)}, f32[32,256]{1,0:T(8,128)S(1)}, s32[32,256]{1,0:T(8,128)S(1)}, f32[3,513]{1,0:T(4,128)S(1)}, f32[3,32,256]{0,2,1:T(8,128)}, /*index=5*/f32[3,256]{0,1:T(8,128)S(1)}) %tuple.225, f32[3,256]{0,1:T(8,128)S(1)} %get-tuple-element.543), branch_computations={%region_23.26_spmd, %region_26.27_spmd} | conditional | flops 238336 | bytes 1860696 | solution.py:198
  402.3 27.9 %gather_fusion = f32[8192,3]{1,0:T(8,128)} fusion(f32[3,513]{0,1:T(8,128)S(1)} %copy.129, s32[8192]{0:T(1024)S(1)} %broadcast_clamp_fusion), kind=kCustom, calls=%fused_computation.2 | custom fusion | bytes 229376 | tf_op jit(solution)/shard_map/cond/branch_0_fun/gather | solution.py:203
  430.2 4.8 multiply_reduce_fusion
  436.1 2.5 subtract_reduce_fusion
  441.3 6.1 collective-permute-start.9
  448.9 36.7 %conditional.13 = (f32[3,256]{0,1:T(8,128)S(1)}) conditional(s32[]{:T(128)} %convert_element_type.76, (f32[256]{0:T(256)S(1)}, f32[32,256]{1,0:T(8,128)S(1)}, s32[32,256]{1,0:T(8,128)S(1)}, f32[3,513]{1,0:T(4,128)S(1)}, f32[3,32,256]{0,2,1:T(8,128)}, /*index=5*/f32[3,256]{0,1:T(8,128)S(1)}) %tuple.226, f32[3,256]{0,1:T(8,128)S(1)} %get-tuple-element.898), branch_computations={%region_27.30_spmd, %region_30.31_spmd} | conditional | flops 238336 | bytes 1860696 | solution.py:198
  449.1 27.9 %gather_fusion.1 = f32[8192,3]{1,0:T(8,128)} fusion(f32[3,513]{0,1:T(8,128)S(1)} %copy.133, s32[8192]{0:T(1024)S(1)} %broadcast_clamp_fusion.1), kind=kCustom, calls=%fused_computation.3 | custom fusion | bytes 229376 | tf_op jit(solution)/shard_map/cond/branch_0_fun/gather | solution.py:203
  477.0 4.8 multiply_reduce_fusion.1
  482.9 2.5 subtract_reduce_fusion.1
  488.1 6.4 collective-permute-start.11
  497.9 6.7 collective-permute-start.3
  504.9 36.6 %conditional.14 = (f32[3,256]{0,1:T(8,128)S(1)}) conditional(s32[]{:T(128)} %convert_element_type.76, (f32[256]{0:T(256)S(1)}, f32[32,256]{1,0:T(8,128)S(1)}, s32[32,256]{1,0:T(8,128)S(1)}, f32[3,513]{1,0:T(4,128)S(1)}, f32[3,32,256]{0,2,1:T(8,128)}, /*index=5*/f32[3,256]{0,1:T(8,128)S(1)}) %tuple.227, f32[3,256]{0,1:T(8,128)S(1)} %get-tuple-element.899), branch_computations={%region_31.34_spmd, %region_34.35_spmd} | conditional | flops 238336 | bytes 1860696 | solution.py:198
  505.1 27.9 %gather_fusion.2 = f32[8192,3]{1,0:T(8,128)} fusion(f32[3,513]{0,1:T(8,128)S(1)} %copy.137, s32[8192]{0:T(1024)S(1)} %broadcast_clamp_fusion.2), kind=kCustom, calls=%fused_computation.4 | custom fusion | bytes 229376 | tf_op jit(solution)/shard_map/cond/branch_0_fun/gather | solution.py:203
  533.0 4.8 multiply_reduce_fusion.2
  538.9 2.5 subtract_reduce_fusion.2
  544.1 6.4 collective-permute-start.13
  555.2 6.4 collective-permute-start.5
  561.6 36.6 %conditional.15 = (f32[3,256]{0,1:T(8,128)S(1)}) conditional(s32[]{:T(128)} %convert_element_type.76, (f32[256]{0:T(256)S(1)}, f32[32,256]{1,0:T(8,128)S(1)}, s32[32,256]{1,0:T(8,128)S(1)}, f32[3,513]{1,0:T(4,128)S(1)}, f32[3,32,256]{0,2,1:T(8,128)}, /*index=5*/f32[3,256]{0,1:T(8,128)S(1)}) %tuple.228, f32[3,256]{0,1:T(8,128)S(1)} %get-tuple-element.900), branch_computations={%region_35.38_spmd, %region_38.39_spmd} | conditional | flops 238336 | bytes 1860696 | solution.py:198
  561.8 27.9 %gather_fusion.3 = f32[8192,3]{1,0:T(8,128)} fusion(f32[3,513]{0,1:T(8,128)S(1)} %copy.141, s32[8192]{0:T(1024)S(1)} %broadcast_clamp_fusion.3), kind=kCustom, calls=%fused_computation.5 | custom fusion | bytes 229376 | tf_op jit(solution)/shard_map/cond/branch_0_fun/gather | solution.py:203
  589.7 4.8 multiply_reduce_fusion.3
  595.6 2.5 subtract_reduce_fusion.3
  602.6 261.5 %all-reduce.2.cloned.1.call-done = f32[3,32768]{1,0:T(4,128)} async-done(((f32[3,32768]{1,0:T(4,128)}), f32[3,32768]{1,0:T(4,128)}) %all-reduce.2.cloned.1.call-update) | async-done | bytes 393232 | tf_op jit(solution)/shard_map/psum | solution.py:218
  864.8 5.2 collective-permute-start.15
  (210 shorter events, 46.6 us)
Async XLA Ops:
  7.2 591.5 %copy-start = (bf16[256,2]{0,1:T(2,128)(2,1)S(1)}, bf16[256,2]{0,1:T(2,128)(2,1)}, u32[]{:S(2)}) copy-start(bf16[256,2]{0,1:T(2,128)(2,1)} %param.51) | copy-start | bytes 3076
  7.2 856.9 %all-reduce.2.cloned.1.call-start = ((), (), s32[]{:S(2)}) async-start(), calls=%async_computation | async-start | bytes 1048576 | tf_op jit(solution)/shard_map/psum | solution.py:218
  8.0 86.1 %collective-permute-start = (f32[5,256]{1,0:T(8,128)S(1)}, f32[5,256]{1,0:T(8,128)S(1)}, u32[]{:S(2)}, u32[]{:S(2)}) collective-permute-start(f32[5,256]{1,0:T(8,128)S(1)} %pad_maximum_fusion), channel_id=1, source_target_pairs={{0,128},{128,0},{1,129},{129,1},{2,130},{130,2},{3,131},{131,3},{4... | collective-permute-start | bytes 15368 | tf_op jit(solution)/shard_map/ppermute | solution.py:31
  12.8 10.5 %collective-permute-start.2 = (f32[5,128]{0,1:T(8,128)S(1)}, f32[5,128]{0,1:T(8,128)S(1)}, u32[]{:S(2)}, u32[]{:S(2)}) collective-permute-start(f32[5,128]{0,1:T(8,128)S(1)} %bitcast.260), channel_id=1, source_target_pairs={{1,0},{2,1},{3,2},{4,3},{5,4},{6,5},{7,6},{8,7},{9,8},{10,9},{11,1... | collective-permute-start | bytes 7688 | tf_op jit(solution)/shard_map/ppermute | solution.py:23
  14.7 8.6 collective-permute-start.1
  89.6 301.4 %copy-start.12 = (f32[3,256]{1,0:T(4,128)S(1)}, f32[3,256]{1,0:T(4,128)}, u32[]{:S(2)}) copy-start(f32[3,256]{1,0:T(4,128)} %param.38) | copy-start | bytes 9220
  391.1 11.0 %copy-start.10 = (s32[256,32]{0,1:T(8,128)S(1)}, s32[256,32]{0,1:T(8,128)}, u32[]{:S(2)}) copy-start(s32[256,32]{0,1:T(8,128)} %param.42) | copy-start | bytes 98308
  393.9 6.9 collective-permute-start.8
  395.2 6.8 collective-permute-start.7
  430.2 5.9 copy-start.6
  440.0 7.5 collective-permute-start.10
  441.3 7.4 collective-permute-start.9
  448.8 45.7 %copy-start.14 = (bf16[256,256]{1,0:T(8,128)(2,1)S(1)}, bf16[256,256]{1,0:T(8,128)(2,1)}, u32[]{:S(2)}) copy-start(bf16[256,256]{1,0:T(8,128)(2,1)} %param.41) | copy-start | bytes 393220
  448.8 45.7 %copy-start.22 = (f32[256]{0:T(256)S(1)}, f32[256]{0:T(256)}, u32[]{:S(2)}) copy-start(f32[256]{0:T(256)} %param.50) | copy-start | bytes 3076
  448.8 45.8 %copy-start.13 = (bf16[2,256,256]{2,1,0:T(8,128)(2,1)S(1)}, bf16[2,256,256]{2,1,0:T(8,128)(2,1)}, u32[]{:S(2)}) copy-start(bf16[2,256,256]{2,1,0:T(8,128)(2,1)} %param.48) | copy-start | bytes 786436
  477.0 4.8 copy-start.3
  477.0 5.9 copy-start.7
  486.8 17.9 %collective-permute-start.12 = (f32[3,128]{0,1:T(8,128)S(1)}, f32[3,128]{0,1:T(8,128)S(1)}, u32[]{:S(2)}, u32[]{:S(2)}) collective-permute-start(f32[3,128]{0,1:T(8,128)S(1)} %bitcast.263), channel_id=1, source_target_pairs={{1,0},{2,1},{3,2},{4,3},{5,4},{6,5},{7,6},{8,7},{9,8},{10,9},{11,1... | collective-permute-start | bytes 4616 | tf_op jit(solution)/shard_map/ppermute | solution.py:23
  488.1 16.7 %collective-permute-start.11 = (f32[3,128]{0,1:T(8,128)S(1)}, f32[3,128]{0,1:T(8,128)S(1)}, u32[]{:S(2)}, u32[]{:S(2)}) collective-permute-start(f32[3,128]{0,1:T(8,128)S(1)} %bitcast.262), channel_id=1, source_target_pairs={{0,1},{1,2},{2,3},{3,4},{4,5},{5,6},{6,7},{7,8},{8,9},{9,10},{10,1... | collective-permute-start | bytes 4616 | tf_op jit(solution)/shard_map/ppermute | solution.py:20
  496.6 55.3 %collective-permute-start.4 = (bf16[128,256]{1,0:T(8,128)(2,1)S(1)}, bf16[128,256]{1,0:T(8,128)(2,1)S(1)}, u32[]{:S(2)}, u32[]{:S(2)}) collective-permute-start(bf16[128,256]{1,0:T(8,128)(2,1)S(1)} %gather_fusion.11), channel_id=1, source_target_pairs={{1,0},{2,1},{3,2},{4,3},{5,4},{6,5},{7,6},{8,7},{9,8},{10,9},{11,1... | collective-permute-start | bytes 196616 | tf_op jit(solution)/shard_map/ppermute | solution.py:23
  497.9 54.0 %collective-permute-start.3 = (bf16[128,256]{1,0:T(8,128)(2,1)S(1)}, bf16[128,256]{1,0:T(8,128)(2,1)S(1)}, u32[]{:S(2)}, u32[]{:S(2)}) collective-permute-start(bf16[128,256]{1,0:T(8,128)(2,1)S(1)} %gather_fusion.10), channel_id=1, source_target_pairs={{0,1},{1,2},{2,3},{3,4},{4,5},{5,6},{6,7},{7,8},{8,9},{9,10},{10,1... | collective-permute-start | bytes 196616 | tf_op jit(solution)/shard_map/ppermute | solution.py:20
  504.9 47.2 %copy-start.15 = (bf16[2,2,64,64]{3,2,1,0:T(8,128)(2,1)S(1)}, bf16[2,2,64,64]{3,2,1,0:T(8,128)(2,1)}, u32[]{:S(2)}) copy-start(bf16[2,2,64,64]{3,2,1,0:T(8,128)(2,1)} %param.46) | copy-start | bytes 98308
  504.9 47.2 %copy-start.16 = (bf16[2,64,256]{2,1,0:T(8,128)(2,1)S(1)}, bf16[2,64,256]{2,1,0:T(8,128)(2,1)}, u32[]{:S(2)}) copy-start(bf16[2,64,256]{2,1,0:T(8,128)(2,1)} %param.47) | copy-start | bytes 196612
  504.9 47.2 %copy-start.19 = (bf16[2,8,64]{2,1,0:T(8,128)(2,1)S(1)}, bf16[2,8,64]{2,1,0:T(8,128)(2,1)}, u32[]{:S(2)}) copy-start(bf16[2,8,64]{2,1,0:T(8,128)(2,1)} %param.45) | copy-start | bytes 6148
  533.0 4.8 copy-start.4
  533.0 5.9 copy-start.8
  542.8 7.9 collective-permute-start.14
  544.1 7.7 collective-permute-start.13
  553.9 44.4 %collective-permute-start.6 = (bf16[128,256]{1,0:T(8,128)(2,1)S(1)}, bf16[128,256]{1,0:T(8,128)(2,1)S(1)}, u32[]{:S(2)}, u32[]{:S(2)}) collective-permute-start(bf16[128,256]{1,0:T(8,128)(2,1)S(1)} %gather_fusion.13), channel_id=1, source_target_pairs={{1,0},{2,1},{3,2},{4,3},{5,4},{6,5},{7,6},{8,7},{9,8},{10,9},{11,1... | collective-permute-start | bytes 196616 | tf_op jit(solution)/shard_map/ppermute | solution.py:23
  555.2 43.1 %collective-permute-start.5 = (bf16[128,256]{1,0:T(8,128)(2,1)S(1)}, bf16[128,256]{1,0:T(8,128)(2,1)S(1)}, u32[]{:S(2)}, u32[]{:S(2)}) collective-permute-start(bf16[128,256]{1,0:T(8,128)(2,1)S(1)} %gather_fusion.12), channel_id=1, source_target_pairs={{0,1},{1,2},{2,3},{3,4},{4,5},{5,6},{6,7},{7,8},{8,9},{9,10},{10,1... | collective-permute-start | bytes 196616 | tf_op jit(solution)/shard_map/ppermute | solution.py:20
  589.7 5.9 copy-start.9
  864.8 6.0 collective-permute-start.15
  (8 other events, 19.4 us)
Sparse Core Ops, SparseCore 0:
  602.7 261.3 all-reduce.1
where the time goes:
time: 879 us; the launch traced here: 878 us
  blocking collectives  296 us (34%)
  waiting for transfers between devices  265 us (30%)
  local copies, waits for them, and re-layouts  195 us (22%)
  starting transfers between devices  60.5 us (7%)
  other arithmetic  45.1 us (5%)
  between operations  14.8 us (2%)
    all_gather x1, blocking collectives, local(): others = lax.all_gather(partner, ('dom', 'sub'), axis=1, tiled=True)  296 us
    psum x1, waiting for transfers between devices, local(): total = lax.psum(scattered, ('dom', 'sub'))  262 us
    gather x4, local copies, waits for them, and re-layouts, local(): t[:, slot_major]  112 us
    ppermute x7, starting transfers between devices, with_halo(): lax.ppermute(lax.slice_in_dim(block, block.shape[dim] - width, None, axis...  43 us
    gather x2, local copies, waits for them, and re-layouts, local(): site_table[3][slot_major]  32.9 us
    gather x1, local copies, waits for them, and re-layouts, local(): offset = positions[:, None, :] - site_table[:3][:, slot_major]  27.9 us
    reduce_sum x5, other arithmetic, slot_field(): projected = jnp.sum(offset * source_dipole, axis=0)  23.5 us
  transfers between devices with their start and end apart: 17, of which 5 were waited for; matrix products, arithmetic and copies ran while one was open for 17% of the time, Pallas kernels for 0%

commit v1 on v0

--- a/solution.py
+++ b/solution.py
@@ -215,7 +215,7 @@
         .add(response_term.reshape(3, listed_count, block_width))
         .reshape(3, -1)
     )
-    total = lax.psum(scattered, ("dom", "sub"))
+    total = lax.psum(lax.psum(scattered, "dom"), "sub")
     own_share = lax.dynamic_slice_in_dim(total, domain_index * row_count, row_count, 1)
     response = partner_2(own_share, "grp", 0)
     return (site_result, response)

time: 879 us -> 1310 us (1.49)
  waiting for transfers between devices: 265 us -> 696 us
    psum x1 -> x2, waiting for transfers between devices: 262 us -> 692 us  [local(): total = lax.psum(lax.psum(scattered, 'dom'), 'sub')]
  transfers between devices with their start and end apart: 17 -> 18, of which waited for: 5 -> 6; matrix products, arithmetic and copies ran while one was open for 17% -> 11% of each run, Pallas kernels for 0% -> 0%
where the time goes in v1:
time: 1310 us; the launch traced here: 1300 us
  waiting for transfers between devices  696 us (53%)
  blocking collectives  296 us (23%)
  local copies, waits for them, and re-layouts  195 us (15%)
  starting transfers between devices  56 us (4%)
  other arithmetic  45.1 us (3%)
  between operations  14.8 us (1%)
    psum x2, waiting for transfers between devices, local(): total = lax.psum(lax.psum(scattered, 'dom'), 'sub')  692 us
    all_gather x1, blocking collectives, local(): others = lax.all_gather(partner, ('dom', 'sub'), axis=1, tiled=True)  296 us
    gather x4, local copies, waits for them, and re-layouts, local(): t[:, slot_major]  112 us
    ppermute x7, starting transfers between devices, with_halo(): lax.ppermute(lax.slice_in_dim(block, block.shape[dim] - width, None, axis...  43 us
    gather x2, local copies, waits for them, and re-layouts, local(): site_table[3][slot_major]  32.9 us
    gather x1, local copies, waits for them, and re-layouts, local(): offset = positions[:, None, :] - site_table[:3][:, slot_major]  27.9 us
  transfers between devices with their start and end apart: 18, of which 6 were waited for; matrix products, arithmetic and copies ran while one was open for 11% of the time, Pallas kernels for 0%

profile of v1, /device:TPU:1, one launch (start us, length us, event | category | flops | bytes accessed | tf_op | source)
XLA Modules:
  0.0 1304.6 jit_solution(12670022668591293518)
XLA Ops:
  8.0 3.2 collective-permute-start
  14.7 5.5 collective-permute-start.1
  24.2 32.9 %gather_fusion.14 = f32[8192]{0:T(1024)S(1)} fusion(f32[513]{0:T(1024)S(1)} %slice_reduce_fusion, s32[8192]{0:T(1024)S(1)} %broadcast_clamp_fusion.4), kind=kCustom, calls=%fused_computation.14 | custom fusion | bytes 98304 | tf_op jit(solution)/shard_map/gather | solution.py:191
  57.2 27.9 %gather_fusion.9 = f32[8192,3]{1,0:T(8,128)} fusion(f32[3,513]{0,1:T(8,128)S(1)} %copy.124, s32[8192]{0:T(1024)S(1)} %broadcast_clamp_fusion.4), kind=kCustom, calls=%fused_computation.9 | custom fusion | bytes 229376 | tf_op jit(solution)/shard_map/gather | solution.py:149
  85.1 4.5 multiply_reduce_fusion.4
  89.6 1.9 copy-done.1
  91.5 2.5 subtract_reduce_fusion.4
  94.0 296.4 %all_gather.3 = f32[5,32768]{1,0:T(8,128)S(1)} all-gather(f32[5,256]{1,0:T(8,128)S(1)} %collective-permute-done), channel_id=1, replica_groups=mesh['grp'=2,'dom'=64,'sub'=2] {'dom','sub'}, dimensions={1}, use_global_device_ids=true | all-gather | bytes 660480 | tf_op jit(solution)/shard_map/all_gather | solution.py:146
  395.2 5.5 collective-permute-start.7
  402.1 36.6 %conditional.12 = (f32[3,256]{0,1:T(8,128)S(1)}) conditional(s32[]{:T(128)} %convert_element_type.76, (f32[256]{0:T(256)S(1)}, f32[32,256]{1,0:T(8,128)S(1)}, s32[32,256]{1,0:T(8,128)S(1)}, f32[3,513]{1,0:T(4,128)S(1)}, f32[3,32,256]{0,2,1:T(8,128)}, /*index=5*/f32[3,256]{0,1:T(8,128)S(1)}) %tuple.227, f32[3,256]{0,1:T(8,128)S(1)} %get-tuple-element.543), branch_computations={%region_23.26_spmd, %region_26.27_spmd} | conditional | flops 238336 | bytes 1860696 | solution.py:198
  402.3 27.9 %gather_fusion = f32[8192,3]{1,0:T(8,128)} fusion(f32[3,513]{0,1:T(8,128)S(1)} %copy.129, s32[8192]{0:T(1024)S(1)} %broadcast_clamp_fusion), kind=kCustom, calls=%fused_computation.2 | custom fusion | bytes 229376 | tf_op jit(solution)/shard_map/cond/branch_0_fun/gather | solution.py:203
  430.2 4.8 multiply_reduce_fusion
  436.1 2.5 subtract_reduce_fusion
  441.3 6.1 collective-permute-start.9
  448.9 36.7 %conditional.13 = (f32[3,256]{0,1:T(8,128)S(1)}) conditional(s32[]{:T(128)} %convert_element_type.76, (f32[256]{0:T(256)S(1)}, f32[32,256]{1,0:T(8,128)S(1)}, s32[32,256]{1,0:T(8,128)S(1)}, f32[3,513]{1,0:T(4,128)S(1)}, f32[3,32,256]{0,2,1:T(8,128)}, /*index=5*/f32[3,256]{0,1:T(8,128)S(1)}) %tuple.228, f32[3,256]{0,1:T(8,128)S(1)} %get-tuple-element.898), branch_computations={%region_27.30_spmd, %region_30.31_spmd} | conditional | flops 238336 | bytes 1860696 | solution.py:198
  449.1 27.9 %gather_fusion.1 = f32[8192,3]{1,0:T(8,128)} fusion(f32[3,513]{0,1:T(8,128)S(1)} %copy.133, s32[8192]{0:T(1024)S(1)} %broadcast_clamp_fusion.1), kind=kCustom, calls=%fused_computation.3 | custom fusion | bytes 229376 | tf_op jit(solution)/shard_map/cond/branch_0_fun/gather | solution.py:203
  477.0 4.8 multiply_reduce_fusion.1
  482.9 2.5 subtract_reduce_fusion.1
  488.1 6.4 collective-permute-start.11
  497.9 6.7 collective-permute-start.3
  504.9 36.6 %conditional.14 = (f32[3,256]{0,1:T(8,128)S(1)}) conditional(s32[]{:T(128)} %convert_element_type.76, (f32[256]{0:T(256)S(1)}, f32[32,256]{1,0:T(8,128)S(1)}, s32[32,256]{1,0:T(8,128)S(1)}, f32[3,513]{1,0:T(4,128)S(1)}, f32[3,32,256]{0,2,1:T(8,128)}, /*index=5*/f32[3,256]{0,1:T(8,128)S(1)}) %tuple.229, f32[3,256]{0,1:T(8,128)S(1)} %get-tuple-element.899), branch_computations={%region_31.34_spmd, %region_34.35_spmd} | conditional | flops 238336 | bytes 1860696 | solution.py:198
  505.1 27.9 %gather_fusion.2 = f32[8192,3]{1,0:T(8,128)} fusion(f32[3,513]{0,1:T(8,128)S(1)} %copy.137, s32[8192]{0:T(1024)S(1)} %broadcast_clamp_fusion.2), kind=kCustom, calls=%fused_computation.4 | custom fusion | bytes 229376 | tf_op jit(solution)/shard_map/cond/branch_0_fun/gather | solution.py:203
  533.0 4.8 multiply_reduce_fusion.2
  538.9 2.5 subtract_reduce_fusion.2
  544.1 6.4 collective-permute-start.13
  555.2 6.4 collective-permute-start.5
  561.6 36.6 %conditional.15 = (f32[3,256]{0,1:T(8,128)S(1)}) conditional(s32[]{:T(128)} %convert_element_type.76, (f32[256]{0:T(256)S(1)}, f32[32,256]{1,0:T(8,128)S(1)}, s32[32,256]{1,0:T(8,128)S(1)}, f32[3,513]{1,0:T(4,128)S(1)}, f32[3,32,256]{0,2,1:T(8,128)}, /*index=5*/f32[3,256]{0,1:T(8,128)S(1)}) %tuple.230, f32[3,256]{0,1:T(8,128)S(1)} %get-tuple-element.900), branch_computations={%region_35.38_spmd, %region_38.39_spmd} | conditional | flops 238336 | bytes 1860696 | solution.py:198
  561.8 27.9 %gather_fusion.3 = f32[8192,3]{1,0:T(8,128)} fusion(f32[3,513]{0,1:T(8,128)S(1)} %copy.141, s32[8192]{0:T(1024)S(1)} %broadcast_clamp_fusion.3), kind=kCustom, calls=%fused_computation.5 | custom fusion | bytes 229376 | tf_op jit(solution)/shard_map/cond/branch_0_fun/gather | solution.py:203
  589.7 4.8 multiply_reduce_fusion.3
  595.6 2.5 subtract_reduce_fusion.3
  602.6 607.4 %all-reduce.3.cloned.1.call-done = f32[3,32768]{1,0:T(4,128)} async-done(((f32[3,32768]{1,0:T(4,128)}), f32[3,32768]{1,0:T(4,128)}) %all-reduce.3.cloned.1.call-update) | async-done | bytes 393232 | tf_op jit(solution)/shard_map/psum | solution.py:218
  1210.0 85.0 %all-reduce.5.cloned.1.call-done = f32[3,32768]{1,0:T(4,128)} async-done(((f32[3,32768]{1,0:T(4,128)}), f32[3,32768]{1,0:T(4,128)}) %all-reduce.5.cloned.1.call-update) | async-done | bytes 393232 | tf_op jit(solution)/shard_map/psum | solution.py:218
  (213 shorter events, 47.3 us)
Async XLA Ops:
  7.2 591.5 %copy-start = (bf16[256,2]{0,1:T(2,128)(2,1)S(1)}, bf16[256,2]{0,1:T(2,128)(2,1)}, u32[]{:S(2)}) copy-start(bf16[256,2]{0,1:T(2,128)(2,1)} %param.51) | copy-start | bytes 3076
  7.2 1202.8 %all-reduce.3.cloned.1.call-start = ((), (), s32[]{:S(2)}) async-start(), calls=%async_computation | async-start | bytes 1048576 | tf_op jit(solution)/shard_map/psum | solution.py:218
  8.0 86.1 %collective-permute-start = (f32[5,256]{1,0:T(8,128)S(1)}, f32[5,256]{1,0:T(8,128)S(1)}, u32[]{:S(2)}, u32[]{:S(2)}) collective-permute-start(f32[5,256]{1,0:T(8,128)S(1)} %pad_maximum_fusion), channel_id=1, source_target_pairs={{0,128},{128,0},{1,129},{129,1},{2,130},{130,2},{3,131},{131,3},{4... | collective-permute-start | bytes 15368 | tf_op jit(solution)/shard_map/ppermute | solution.py:31
  12.8 10.5 collective-permute-start.2
  14.7 8.6 collective-permute-start.1
  89.6 301.4 %copy-start.12 = (f32[3,256]{1,0:T(4,128)S(1)}, f32[3,256]{1,0:T(4,128)}, u32[]{:S(2)}) copy-start(f32[3,256]{1,0:T(4,128)} %param.38) | copy-start | bytes 9220
  391.1 11.0 copy-start.10
  393.9 6.9 collective-permute-start.8
  395.2 6.8 collective-permute-start.7
  430.2 5.9 copy-start.6
  440.0 7.5 collective-permute-start.10
  441.3 7.4 collective-permute-start.9
  448.8 45.7 %copy-start.14 = (bf16[256,256]{1,0:T(8,128)(2,1)S(1)}, bf16[256,256]{1,0:T(8,128)(2,1)}, u32[]{:S(2)}) copy-start(bf16[256,256]{1,0:T(8,128)(2,1)} %param.41) | copy-start | bytes 393220
  448.8 45.7 %copy-start.22 = (f32[256]{0:T(256)S(1)}, f32[256]{0:T(256)}, u32[]{:S(2)}) copy-start(f32[256]{0:T(256)} %param.50) | copy-start | bytes 3076
  448.8 45.8 %copy-start.13 = (bf16[2,256,256]{2,1,0:T(8,128)(2,1)S(1)}, bf16[2,256,256]{2,1,0:T(8,128)(2,1)}, u32[]{:S(2)}) copy-start(bf16[2,256,256]{2,1,0:T(8,128)(2,1)} %param.48) | copy-start | bytes 786436
  477.0 4.8 copy-start.3
  477.0 5.9 copy-start.7
  486.8 17.9 %collective-permute-start.12 = (f32[3,128]{0,1:T(8,128)S(1)}, f32[3,128]{0,1:T(8,128)S(1)}, u32[]{:S(2)}, u32[]{:S(2)}) collective-permute-start(f32[3,128]{0,1:T(8,128)S(1)} %bitcast.263), channel_id=1, source_target_pairs={{1,0},{2,1},{3,2},{4,3},{5,4},{6,5},{7,6},{8,7},{9,8},{10,9},{11,1... | collective-permute-start | bytes 4616 | tf_op jit(solution)/shard_map/ppermute | solution.py:23
  488.1 16.7 %collective-permute-start.11 = (f32[3,128]{0,1:T(8,128)S(1)}, f32[3,128]{0,1:T(8,128)S(1)}, u32[]{:S(2)}, u32[]{:S(2)}) collective-permute-start(f32[3,128]{0,1:T(8,128)S(1)} %bitcast.262), channel_id=1, source_target_pairs={{0,1},{1,2},{2,3},{3,4},{4,5},{5,6},{6,7},{7,8},{8,9},{9,10},{10,1... | collective-permute-start | bytes 4616 | tf_op jit(solution)/shard_map/ppermute | solution.py:20
  496.6 55.3 %collective-permute-start.4 = (bf16[128,256]{1,0:T(8,128)(2,1)S(1)}, bf16[128,256]{1,0:T(8,128)(2,1)S(1)}, u32[]{:S(2)}, u32[]{:S(2)}) collective-permute-start(bf16[128,256]{1,0:T(8,128)(2,1)S(1)} %gather_fusion.11), channel_id=1, source_target_pairs={{1,0},{2,1},{3,2},{4,3},{5,4},{6,5},{7,6},{8,7},{9,8},{10,9},{11,1... | collective-permute-start | bytes 196616 | tf_op jit(solution)/shard_map/ppermute | solution.py:23
  497.9 54.0 %collective-permute-start.3 = (bf16[128,256]{1,0:T(8,128)(2,1)S(1)}, bf16[128,256]{1,0:T(8,128)(2,1)S(1)}, u32[]{:S(2)}, u32[]{:S(2)}) collective-permute-start(bf16[128,256]{1,0:T(8,128)(2,1)S(1)} %gather_fusion.10), channel_id=1, source_target_pairs={{0,1},{1,2},{2,3},{3,4},{4,5},{5,6},{6,7},{7,8},{8,9},{9,10},{10,1... | collective-permute-start | bytes 196616 | tf_op jit(solution)/shard_map/ppermute | solution.py:20
  504.9 47.2 %copy-start.15 = (bf16[2,2,64,64]{3,2,1,0:T(8,128)(2,1)S(1)}, bf16[2,2,64,64]{3,2,1,0:T(8,128)(2,1)}, u32[]{:S(2)}) copy-start(bf16[2,2,64,64]{3,2,1,0:T(8,128)(2,1)} %param.46) | copy-start | bytes 98308
  504.9 47.2 %copy-start.16 = (bf16[2,64,256]{2,1,0:T(8,128)(2,1)S(1)}, bf16[2,64,256]{2,1,0:T(8,128)(2,1)}, u32[]{:S(2)}) copy-start(bf16[2,64,256]{2,1,0:T(8,128)(2,1)} %param.47) | copy-start | bytes 196612
  504.9 47.2 %copy-start.19 = (bf16[2,8,64]{2,1,0:T(8,128)(2,1)S(1)}, bf16[2,8,64]{2,1,0:T(8,128)(2,1)}, u32[]{:S(2)}) copy-start(bf16[2,8,64]{2,1,0:T(8,128)(2,1)} %param.45) | copy-start | bytes 6148
  533.0 5.9 copy-start.8
  542.8 7.9 collective-permute-start.14
  544.1 7.7 collective-permute-start.13
  553.9 44.4 %collective-permute-start.6 = (bf16[128,256]{1,0:T(8,128)(2,1)S(1)}, bf16[128,256]{1,0:T(8,128)(2,1)S(1)}, u32[]{:S(2)}, u32[]{:S(2)}) collective-permute-start(bf16[128,256]{1,0:T(8,128)(2,1)S(1)} %gather_fusion.13), channel_id=1, source_target_pairs={{1,0},{2,1},{3,2},{4,3},{5,4},{6,5},{7,6},{8,7},{9,8},{10,9},{11,1... | collective-permute-start | bytes 196616 | tf_op jit(solution)/shard_map/ppermute | solution.py:23
  555.2 43.1 %collective-permute-start.5 = (bf16[128,256]{1,0:T(8,128)(2,1)S(1)}, bf16[128,256]{1,0:T(8,128)(2,1)S(1)}, u32[]{:S(2)}, u32[]{:S(2)}) collective-permute-start(bf16[128,256]{1,0:T(8,128)(2,1)S(1)} %gather_fusion.12), channel_id=1, source_target_pairs={{0,1},{1,2},{2,3},{3,4},{4,5},{5,6},{6,7},{7,8},{8,9},{9,10},{10,1... | collective-permute-start | bytes 196616 | tf_op jit(solution)/shard_map/ppermute | solution.py:20
  589.7 5.9 copy-start.9
  602.5 692.5 %all-reduce.5.cloned.1.call-start = ((), (), s32[]{:S(2)}) async-start(), calls=%async_computation.1 | async-start | bytes 1048576 | tf_op jit(solution)/shard_map/psum | solution.py:218
  1295.7 1.5 collective-permute-start.15
  (9 other events, 24.1 us)
Sparse Core Ops, SparseCore 0:
  602.7 607.2 all-reduce.2
  1212.8 82.1 all-reduce.4
